TPU v7x, 256 devices: a whole 4x4x8 slice. The times are simulated.
256 devices in a mesh: band: 32 (over y_hi, z, core), fft: 8 (over y_lo, x).
Axes of the slice: x: 4, y: 4 (y_hi: 2, y_lo: 2; y = y_hi * 2 + y_lo), z: 8, core: 2. Of those that a mesh axis runs over, the one named last changes fastest.
Arguments:
- orbitals: float32 [64, 96, 9216], P('band', 'fft'), may hold values from -6 to 6
- owners: int32 [1], replicated, may hold values from 0 to 31
- cutoff_mask: int32 [96, 9216], P(None, 'fft'), may hold values from 0 to 1, as said below
Outputs:
- exchange_local: float32 [64, 96, 9216], P('band', 'fft')
- exchange_block: float32 [2, 96, 9216], P(None, 'fft')
Inputs may be any that keep to these rules, and one draw needn't show every extreme that they name: cutoff_mask is 1 exactly at the frequencies whose squared length s(x)^2 + s(y)^2 + s(z)^2 lies between 1 and a cutoff, and 0 elsewhere (0 at frequency (0, 0, 0)); it is unchanged when the sign of any one frequency component is changed.
All inputs are finite; a program needn't handle non-finite values.
Results may differ from a plain program's by a relative error of at most 0.00029.
Values sent between devices are 32-bit elements; how exact they have to be, the bound alone decides.
A program may use at most 128 MiB of HBM per device.

v0:
```python
import math
import jax
import jax.numpy as jnp
from jax import lax
from jax.sharding import PartitionSpec as P

COULOMB = 400.0
EXCHANGE_MIX = 0.25


def broadcast(value, axis, source):
    kept = jnp.where(lax.axis_index(axis) == source, value, 0).astype(value.dtype)
    return lax.psum(kept, axis)


def dft_tables(count):
    positions = jnp.arange(count, dtype=jnp.int32)
    phases = positions[:, None] * positions[None, :] % count
    angles = phases.astype(jnp.float32) * (2.0 * math.pi / count)
    return (jnp.cos(angles), jnp.sin(angles))


def transform_dim(values, matrix, dim):
    source = "pabc"
    target = source[:dim] + "k" + source[dim + 1 :]
    pattern = source + "," + source[dim] + "k" + "->" + target
    return jnp.einsum(pattern, values, matrix, precision=lax.Precision.HIGHEST)


def forward_local(real_data, cosine, sine):
    casine = cosine + sine
    parts = [transform_dim(transform_dim(real_data, casine, 3), casine, 2)]
    stacked = jnp.stack(parts, axis=1)
    return stacked.reshape(stacked.shape[0], stacked.shape[1], stacked.shape[2], -1)


def spectral_middle(spectrum, kernel, cosine, sine):
    count_pairs, components, grid_size, flat_cells = spectrum.shape
    shaped = spectrum.reshape(count_pairs, components, grid_size, kernel.shape[1], grid_size)
    casine = cosine + sine
    scaled = transform_dim(shaped[:, 0], casine, 1) * kernel
    parts = [transform_dim(scaled, casine, 1)]
    return jnp.stack(parts, axis=1).reshape(count_pairs, components, grid_size, flat_cells)


def inverse_local(spectrum, cosine, sine):
    count_pairs, components, slab_rows, flat_cells = spectrum.shape
    grid_size = cosine.shape[0]
    shaped = spectrum.reshape(count_pairs, components, slab_rows, grid_size, grid_size)
    casine = cosine + sine
    result = transform_dim(transform_dim(shaped[:, 0], casine, 2), casine, 3)
    result = result / float(grid_size * grid_size * grid_size)
    return result.reshape(count_pairs, slab_rows, flat_cells)


def per_device(orbitals, owners, cutoff_mask):
    local_bands, slab_rows, flat_cells = orbitals.shape
    grid_size = slab_rows * lax.axis_size("fft")
    cosine, sine = dft_tables(grid_size)
    positions = jnp.arange(grid_size, dtype=jnp.int32)
    signed = jnp.where(positions <= grid_size // 2, positions, positions - grid_size)
    signed_y = lax.dynamic_slice_in_dim(signed, lax.axis_index("fft") * slab_rows, slab_rows)
    squared = (
        signed[:, None, None] * signed[:, None, None]
        + signed_y[None, :, None] * signed_y[None, :, None]
        + signed[None, None, :] * signed[None, None, :]
    )
    weights = cutoff_mask.reshape(grid_size, slab_rows, grid_size).astype(jnp.float32)
    kernel = COULOMB * weights / jnp.maximum(squared, 1).astype(jnp.float32)
    local_total = jnp.zeros((local_bands, slab_rows, flat_cells), jnp.float32)
    block_orbs = broadcast(orbitals, "band", owners[0])
    pair_data = (orbitals[:, None] * block_orbs[None]).reshape(
        local_bands * local_bands, slab_rows, grid_size, grid_size
    )
    spectrum = forward_local(pair_data, cosine, sine)

    def one_pair(single):
        sent = lax.all_to_all(single[None], "fft", split_axis=3, concat_axis=2, tiled=True)
        pencil_out = spectral_middle(sent, kernel, cosine, sine)
        return lax.all_to_all(pencil_out, "fft", split_axis=2, concat_axis=3, tiled=True)[0]

    returned = lax.map(one_pair, spectrum)
    potential = inverse_local(returned, cosine, sine).reshape(
        local_bands, local_bands, slab_rows, flat_cells
    )
    local_total = local_total - EXCHANGE_MIX * jnp.sum(block_orbs[None] * potential, axis=1)
    block_terms = -EXCHANGE_MIX * jnp.sum(orbitals[:, None] * potential, axis=0)
    block_total = lax.psum(block_terms, "band")
    return (local_total, block_total)


def solution(mesh):
    in_specs = (P("band", "fft", None), P(), P(None, "fft"))
    out_specs = (P("band", "fft", None), P(None, "fft", None))
    return jax.shard_map(
        per_device, mesh=mesh, in_specs=in_specs, out_specs=out_specs, check_vma=False
    )
```

profile of v0, /device:TPU:1, one launch (start us, length us, event | category | flops | bytes accessed | tf_op | source)
XLA Modules:
  0.0 1006.4 jit_solution(8958187725105323984)
XLA Ops:
  10.0 267.7 %all-reduce.3.cloned.1.call-done = f32[2,12,9216]{2,0,1:T(2,128)} async-done(((f32[2,12,9216]{2,0,1:T(2,128)}), f32[2,12,9216]{2,0,1:T(2,128)}) %all-reduce.3.cloned.1.call-update) | async-done | bytes 884752 | tf_op jit(solution)/shard_map/psum | solution.py:13
  284.6 3.9 fusion.23
  292.4 12.8 %copy.59 = f32[4,12,96,96]{1,0,3,2:T(4,128)} copy(f32[4,12,96,96]{3,2,1,0:T(8,128)} %convolution_bitcast_fusion.1) | data formatting | bytes 3538944
  305.2 395.2 %while.14 = (s32[]{:T(128)}, f32[4,1,12,9216]{3,1,2,0:T(1,128)}, f32[4,1,12,9216]{2,1,0,3:T(1,128)}, f32[96,12,96]{0,2,1:T(8,128)S(1)}, s32[]{:T(128)}, /*index=5*/f32[]{:T(128)}, f32[]{:T(128)}) while((s32[]{:T(128)}, f32[4,1,12,9216]{3,1,2,0:T(1,128)}, f32[4,1,12,9216]{2,1,0,3:T(1,128)}, f32[96,12,96]{0,2,1:T(8,128)S(1)}, ...), condition=%wide.region_2.3_spmd.clone.clone, body=%wide.region_1.2_spmd.clone.clone.sunk | while | flops 255098880 | bytes 14155925 | solution.py:82
  317.5 4.9 fusion.62
  322.9 43.0 %reduce.5 = f32[9216,12]{1,0:T(8,128)} reduce(f32[9216,1,1,12]{3,2,1,0:T(1,128)} %fusion.62, f32[]{:T(128)} %broadcast.59), dimensions={1,2}, to_apply=%fusion.51.reduce_sub_computation | reduce | bytes 884740 | tf_op jit(solution)/shard_map/while
  365.9 6.0 reshape.105
  371.9 11.1 %all_to_all.58 = f32[8,1,13824]{2,1,0:T(1,128)S(1)} all-to-all(f32[8,1,13824]{2,1,0:T(1,128)S(1)} %reshape.105), channel_id=1, replica_groups=mesh['band'=32,'fft'=8] {'fft'}, dimensions={0} | all-to-all | bytes 884736 | tf_op jit(solution)/shard_map/while/body/eval_jaxpr/all_to_all | solution.py:78
  385.2 10.4 %reshape.106 = f32[9216,1,1,12]{3,2,1,0:T(1,128)} reshape(f32[8,13824]{1,0:T(8,128)S(1)} %reduce.6) | data formatting | bytes 884736 | tf_op jit(solution)/shard_map/while
  406.5 7.0 all-to-all-done.1
  414.4 4.8 fusion.62
  419.8 43.0 %reduce.5 = f32[9216,12]{1,0:T(8,128)} reduce(f32[9216,1,1,12]{3,2,1,0:T(1,128)} %fusion.62, f32[]{:T(128)} %broadcast.59), dimensions={1,2}, to_apply=%fusion.51.reduce_sub_computation | reduce | bytes 884740 | tf_op jit(solution)/shard_map/while
  462.8 6.0 reshape.105
  468.8 9.6 all_to_all.58
  480.6 10.4 %reshape.106 = f32[9216,1,1,12]{3,2,1,0:T(1,128)} reshape(f32[8,13824]{1,0:T(8,128)S(1)} %reduce.6) | data formatting | bytes 884736 | tf_op jit(solution)/shard_map/while
  501.9 7.0 all-to-all-done.1
  509.8 4.8 fusion.62
  515.2 43.0 %reduce.5 = f32[9216,12]{1,0:T(8,128)} reduce(f32[9216,1,1,12]{3,2,1,0:T(1,128)} %fusion.62, f32[]{:T(128)} %broadcast.59), dimensions={1,2}, to_apply=%fusion.51.reduce_sub_computation | reduce | bytes 884740 | tf_op jit(solution)/shard_map/while
  558.2 6.0 reshape.105
  564.2 9.5 all_to_all.58
  575.9 10.4 %reshape.106 = f32[9216,1,1,12]{3,2,1,0:T(1,128)} reshape(f32[8,13824]{1,0:T(8,128)S(1)} %reduce.6) | data formatting | bytes 884736 | tf_op jit(solution)/shard_map/while
  597.2 7.0 all-to-all-done.1
  605.1 4.8 fusion.62
  610.5 43.0 %reduce.5 = f32[9216,12]{1,0:T(8,128)} reduce(f32[9216,1,1,12]{3,2,1,0:T(1,128)} %fusion.62, f32[]{:T(128)} %broadcast.59), dimensions={1,2}, to_apply=%fusion.51.reduce_sub_computation | reduce | bytes 884740 | tf_op jit(solution)/shard_map/while
  653.5 6.0 reshape.105
  659.5 9.5 all_to_all.58
  671.2 10.4 %reshape.106 = f32[9216,1,1,12]{3,2,1,0:T(1,128)} reshape(f32[8,13824]{1,0:T(8,128)S(1)} %reduce.6) | data formatting | bytes 884736 | tf_op jit(solution)/shard_map/while
  692.5 7.0 all-to-all-done.1
  700.4 5.7 reduce
  708.2 4.0 fusion.33
  716.9 8.7 multiply_reduce_fusion
  728.3 268.7 %all-reduce.5.cloned.1.call-done = f32[2,12,9216]{2,0,1:T(2,128)} async-done(((f32[2,12,9216]{2,0,1:T(2,128)}), f32[2,12,9216]{2,0,1:T(2,128)}) %all-reduce.5.cloned.1.call-update) | async-done | bytes 884752 | tf_op jit(solution)/shard_map/psum | solution.py:88
  (74 shorter events, 82.2 us)
Async XLA Ops:
  7.2 2.1 copy-start.1
  7.2 270.5 %all-reduce.3.cloned.1.call-start = ((), (), s32[]{:S(2)}) async-start(), calls=%async_computation.2 | async-start | bytes 1769472 | tf_op jit(solution)/shard_map/psum | solution.py:13
  9.2 268.4 %copy-start = (f32[2,12,9216]{2,0,1:T(2,128)S(1)}, f32[2,12,9216]{2,0,1:T(2,128)}, u32[]{:S(2)}) copy-start(f32[2,12,9216]{2,0,1:T(2,128)} %param.5) | copy-start | bytes 2654212
  9.2 987.7 %all-reduce.5.cloned.1.call-start = ((), (), s32[]{:S(2)}) async-start(), calls=%async_computation.3 | async-start | bytes 1769472 | tf_op jit(solution)/shard_map/psum | solution.py:88
  403.0 10.5 %all-to-all-start.1 = ((f32[1,1,96,1152]{3,1,0,2:T(1,128)}), f32[1,1,96,1152]{3,1,0,2:T(1,128)S(1)}, u32[]{:S(2)}, u32[]{:S(2)}) async-start(f32[1,1,96,1152]{3,1,0,2:T(1,128)} %copy.75), calls=%async_computation.1 | async-start | bytes 884736 | tf_op jit(solution)/shard_map/while/body/eval_jaxpr/all_to_all | solution.py:80
  498.4 10.5 %all-to-all-start.1 = ((f32[1,1,96,1152]{3,1,0,2:T(1,128)}), f32[1,1,96,1152]{3,1,0,2:T(1,128)S(1)}, u32[]{:S(2)}, u32[]{:S(2)}) async-start(f32[1,1,96,1152]{3,1,0,2:T(1,128)} %copy.75), calls=%async_computation.1 | async-start | bytes 884736 | tf_op jit(solution)/shard_map/while/body/eval_jaxpr/all_to_all | solution.py:80
  593.7 10.5 %all-to-all-start.1 = ((f32[1,1,96,1152]{3,1,0,2:T(1,128)}), f32[1,1,96,1152]{3,1,0,2:T(1,128)S(1)}, u32[]{:S(2)}, u32[]{:S(2)}) async-start(f32[1,1,96,1152]{3,1,0,2:T(1,128)} %copy.75), calls=%async_computation.1 | async-start | bytes 884736 | tf_op jit(solution)/shard_map/while/body/eval_jaxpr/all_to_all | solution.py:80
  689.0 10.5 %all-to-all-start.1 = ((f32[1,1,96,1152]{3,1,0,2:T(1,128)}), f32[1,1,96,1152]{3,1,0,2:T(1,128)S(1)}, u32[]{:S(2)}, u32[]{:S(2)}) async-start(f32[1,1,96,1152]{3,1,0,2:T(1,128)} %copy.75), calls=%async_computation.1 | async-start | bytes 884736 | tf_op jit(solution)/shard_map/while/body/eval_jaxpr/all_to_all | solution.py:80
Sparse Core Ops, SparseCore 0:
  11.2 266.4 all-reduce.2
  727.0 269.8 all-reduce.4
where the time goes:
time: 1010 us
  waiting for transfers between devices  565 us (56%)
  other arithmetic  201 us (20%)
  local copies, waits for them, and re-layouts  136 us (13%)
  blocking collectives  39.7 us (4%)
  matrix products  23.2 us (2%)
  between operations  15.3 us (2%)
  starting transfers between devices  14 us (1%)
  loops' own time  12.6 us (1%)
    psum x1, waiting for transfers between devices, per_device(): block_total = lax.psum(block_terms, 'band')  269 us
    psum x1, waiting for transfers between devices, broadcast(): return lax.psum(kept, axis)  268 us
    while x4, other arithmetic  172 us
    while x16, local copies, waits for them, and re-layouts  86.9 us
    all_to_all x4, blocking collectives, one_pair(): lax.all_to_all(single[None], 'fft', split_axis=3, concat_axis=2, tiled=True)  39.7 us
    all_to_all x4, waiting for transfers between devices, one_pair(): lax.all_to_all(pencil_out, 'fft', split_axis=2, concat_axis=3, tiled=True)  28.1 us
    dot_general x12, matrix products, transform_dim(): return jnp.einsum(pattern, values, matrix, precision=lax.Precision.HIGHEST)  23.2 us
  transfers between devices with their start and end apart: 6, of which 6 were waited for; matrix products, arithmetic and copies ran while one was open for 0% of the time, Pallas kernels for 0%

commit v1 on v0

--- a/solution.py
+++ b/solution.py
@@ -75,7 +75,10 @@
     spectrum = forward_local(pair_data, cosine, sine)
 
     def one_pair(single):
-        sent = lax.all_to_all(single[None], "fft", split_axis=3, concat_axis=2, tiled=True)
+        part = single[None]
+        shards = jnp.split(part, lax.axis_size("fft"), axis=3)
+        incoming = lax.all_to_all(jnp.stack(shards), "fft", 0, 0)
+        sent = jnp.concatenate(incoming, axis=2)
         pencil_out = spectral_middle(sent, kernel, cosine, sine)
         return lax.all_to_all(pencil_out, "fft", split_axis=2, concat_axis=3, tiled=True)[0]
 

time: 1010 us -> 743 us (0.74)
  other arithmetic: 201 us -> 26 us
  local copies, waits for them, and re-layouts: 136 us -> 62 us
  loops' own time: 12.6 us -> 0.21 us
    while x4 -> x0, other arithmetic: 172 us -> none
    while x16 -> x28, local copies, waits for them, and re-layouts: 86.9 us -> 31.3 us
    all_to_all x12 -> x0, local copies, waits for them, and re-layouts: 15.9 us -> none  [one_pair(): lax.all_to_all(single[None], 'fft', split_axis=3, concat_axis=2, tiled=True)]
    unnamed x6 -> x7, local copies, waits for them, and re-layouts: 15 us -> 2.15 us
    another operation x1, loops' own time: 12.6 us -> 0.21 us  [per_device(): returned = lax.map(one_pair, spectrum)]
    another operation x4 -> x10, local copies, waits for them, and re-layouts: 1.72 us -> 12.7 us  [the longest x2 6.46 us: forward_local(): stacked.reshape(stacked.shape[0], stacked.shape[1], stacked.shape[2], -1)]
where the time goes in v1:
time: 743 us; the launch traced here: 741 us
  waiting for transfers between devices  565 us (76%)
  local copies, waits for them, and re-layouts  62 us (8%)
  blocking collectives  39.7 us (5%)
  other arithmetic  26 us (3%)
  matrix products  20.2 us (3%)
  between operations  14.9 us (2%)
  starting transfers between devices  14 us (2%)
    psum x1, waiting for transfers between devices, per_device(): block_total = lax.psum(block_terms, 'band')  269 us
    psum x1, waiting for transfers between devices, broadcast(): return lax.psum(kept, axis)  268 us
    all_to_all x4, blocking collectives, one_pair(): incoming = lax.all_to_all(jnp.stack(shards), 'fft', 0, 0)  39.7 us
    while x28, local copies, waits for them, and re-layouts  31.3 us
    all_to_all x4, waiting for transfers between devices, one_pair(): lax.all_to_all(pencil_out, 'fft', split_axis=2, concat_axis=3, tiled=True)  28.1 us
    dot_general x12, matrix products, transform_dim(): return jnp.einsum(pattern, values, matrix, precision=lax.Precision.HIGHEST)  20.2 us
  transfers between devices with their start and end apart: 6, of which 6 were waited for; matrix products, arithmetic and copies ran while one was open for 0% of the time, Pallas kernels for 0%

profile of v1, /device:TPU:1, one launch (start us, length us, event | category | flops | bytes accessed | tf_op | source)
XLA Modules:
  0.0 741.3 jit_solution(6524608287483820901)
XLA Ops:
  10.0 267.7 %all-reduce.3.cloned.1.call-done = f32[2,12,9216]{2,0,1:T(2,128)} async-done(((f32[2,12,9216]{2,0,1:T(2,128)}), f32[2,12,9216]{2,0,1:T(2,128)}) %all-reduce.3.cloned.1.call-update) | async-done | bytes 884752 | tf_op jit(solution)/shard_map/psum | solution.py:13
  277.6 3.3 broadcast_multiply_fusion
  280.9 2.7 mul.147
  283.6 2.3 fusion.31
  285.9 2.4 convolution_bitcast_fusion.1
  288.3 2.5 reshape.95
  290.8 4.0 copy.43
  294.8 141.3 %while.14 = (s32[]{:T(128)}, f32[4,1,12,9216]{3,1,2,0:T(1,128)}, f32[4,1,12,9216]{3,0,2,1:T(4,128)}, f32[96,12,96]{0,2,1:T(8,128)S(1)}, s32[]{:T(128)}, /*index=...) while((s32[]{:T(128)}, f32[4,1,12,9216]{3,1,2,0:T(1,128)}, ...), condition=%wide.region_2.3_spmd.clone.clone, body=%wide.region_1.2_spmd.clone.clone.sunk | while | flops 255098880 | bytes 9732421 | solution.py:85
  303.8 11.1 %all_to_all.42 = f32[8,1,1,12,1152]{4,2,3,1,0:T(1,128)S(1)} all-to-all(f32[8,1,1,12,1152]{4,2,3,1,0:T(1,128)S(1)} %fusion.83), channel_id=1, replica_groups=mesh['band'=32,'fft'=8] {'fft'}, dimensions={0} | all-to-all | bytes 884736 | tf_op jit(solution)/shard_map/while/body/eval_jaxpr/all_to_all | solution.py:80
  316.3 1.3 convolution_multiply_fusion.2
  319.9 3.5 all-to-all-start.1
  323.3 7.0 all-to-all-done.1
  340.2 9.6 %all_to_all.42 = f32[8,1,1,12,1152]{4,2,3,1,0:T(1,128)S(1)} all-to-all(f32[8,1,1,12,1152]{4,2,3,1,0:T(1,128)S(1)} %fusion.83), channel_id=1, replica_groups=mesh['band'=32,'fft'=8] {'fft'}, dimensions={0} | all-to-all | bytes 884736 | tf_op jit(solution)/shard_map/while/body/eval_jaxpr/all_to_all | solution.py:80
  351.4 1.3 convolution_multiply_fusion.2
  354.9 3.5 all-to-all-start.1
  358.4 7.0 all-to-all-done.1
  375.3 9.5 %all_to_all.42 = f32[8,1,1,12,1152]{4,2,3,1,0:T(1,128)S(1)} all-to-all(f32[8,1,1,12,1152]{4,2,3,1,0:T(1,128)S(1)} %fusion.83), channel_id=1, replica_groups=mesh['band'=32,'fft'=8] {'fft'}, dimensions={0} | all-to-all | bytes 884736 | tf_op jit(solution)/shard_map/while/body/eval_jaxpr/all_to_all | solution.py:80
  386.3 1.3 convolution_multiply_fusion.2
  389.8 3.5 all-to-all-start.1
  393.3 7.0 all-to-all-done.1
  410.1 9.5 %all_to_all.42 = f32[8,1,1,12,1152]{4,2,3,1,0:T(1,128)S(1)} all-to-all(f32[8,1,1,12,1152]{4,2,3,1,0:T(1,128)S(1)} %fusion.83), channel_id=1, replica_groups=mesh['band'=32,'fft'=8] {'fft'}, dimensions={0} | all-to-all | bytes 884736 | tf_op jit(solution)/shard_map/while/body/eval_jaxpr/all_to_all | solution.py:80
  424.7 3.5 all-to-all-start.1
  428.2 7.0 all-to-all-done.1
  436.1 5.7 reduce.1
  441.8 2.0 reshape.96
  443.8 4.0 fusion.41
  447.9 2.2 fusion.33
  450.1 2.5 reshape.97
  452.6 8.4 %multiply_reduce_fusion = (f32[2,12,9216]{2,0,1:T(2,128)S(1)}, f32[2,12,9216]{2,0,1:T(2,128)S(1)}) fusion(f32[2,2,12,9216]{3,2,1,0:T(8,128)} %reshape.97, f32[2,12,9216]{2,0,1:T(2,128)S(1)} %copy-done.1, f32[2,12,9216]{2,0,1:T(2,128)} %all-reduce.3.cloned.1.call-done), kind=kLoop, calls=%fused_computation.46 | loop fusion | flops 1327104 | bytes 5308416 | tf_op jit(solution)/shard_map/reduce_sum | solution.py:90
  462.3 1.4 multiply_subtract_fusion
  463.7 268.7 %all-reduce.5.cloned.1.call-done = f32[2,12,9216]{2,0,1:T(2,128)} async-done(((f32[2,12,9216]{2,0,1:T(2,128)}), f32[2,12,9216]{2,0,1:T(2,128)}) %all-reduce.5.cloned.1.call-update) | async-done | bytes 884752 | tf_op jit(solution)/shard_map/psum | solution.py:91
  732.4 2.1 copy.76
  (77 shorter events, 58.7 us)
Async XLA Ops:
  7.2 2.1 copy-start.2
  7.2 270.5 %all-reduce.3.cloned.1.call-start = ((), (), s32[]{:S(2)}) async-start(), calls=%async_computation.2 | async-start | bytes 1769472 | tf_op jit(solution)/shard_map/psum | solution.py:13
  9.2 268.4 %copy-start = (f32[2,12,9216]{2,0,1:T(2,128)S(1)}, f32[2,12,9216]{2,0,1:T(2,128)}, u32[]{:S(2)}) copy-start(f32[2,12,9216]{2,0,1:T(2,128)} %param.5) | copy-start | bytes 2654212
  9.2 723.1 %all-reduce.5.cloned.1.call-start = ((), (), s32[]{:S(2)}) async-start(), calls=%async_computation.3 | async-start | bytes 1769472 | tf_op jit(solution)/shard_map/psum | solution.py:91
  319.9 10.5 %all-to-all-start.1 = ((f32[1,1,96,1152]{3,1,0,2:T(1,128)}), f32[1,1,96,1152]{3,1,0,2:T(1,128)S(1)}, u32[]{:S(2)}, u32[]{:S(2)}) async-start(f32[1,1,96,1152]{3,1,0,2:T(1,128)} %copy.57), calls=%async_computation.1 | async-start | bytes 884736 | tf_op jit(solution)/shard_map/while/body/eval_jaxpr/all_to_all | solution.py:83
  354.9 10.5 %all-to-all-start.1 = ((f32[1,1,96,1152]{3,1,0,2:T(1,128)}), f32[1,1,96,1152]{3,1,0,2:T(1,128)S(1)}, u32[]{:S(2)}, u32[]{:S(2)}) async-start(f32[1,1,96,1152]{3,1,0,2:T(1,128)} %copy.57), calls=%async_computation.1 | async-start | bytes 884736 | tf_op jit(solution)/shard_map/while/body/eval_jaxpr/all_to_all | solution.py:83
  389.8 10.5 %all-to-all-start.1 = ((f32[1,1,96,1152]{3,1,0,2:T(1,128)}), f32[1,1,96,1152]{3,1,0,2:T(1,128)S(1)}, u32[]{:S(2)}, u32[]{:S(2)}) async-start(f32[1,1,96,1152]{3,1,0,2:T(1,128)} %copy.57), calls=%async_computation.1 | async-start | bytes 884736 | tf_op jit(solution)/shard_map/while/body/eval_jaxpr/all_to_all | solution.py:83
  424.7 10.5 %all-to-all-start.1 = ((f32[1,1,96,1152]{3,1,0,2:T(1,128)}), f32[1,1,96,1152]{3,1,0,2:T(1,128)S(1)}, u32[]{:S(2)}, u32[]{:S(2)}) async-start(f32[1,1,96,1152]{3,1,0,2:T(1,128)} %copy.57), calls=%async_computation.1 | async-start | bytes 884736 | tf_op jit(solution)/shard_map/while/body/eval_jaxpr/all_to_all | solution.py:83
  450.1 2.5 copy-start.1
Sparse Core Ops, SparseCore 0:
  11.2 266.4 all-reduce.2
  462.4 269.8 all-reduce.4
